TPU v7x, 512 devices: a whole 4x4x16 slice. The times are simulated.
512 devices in a mesh: buyers: 32 (over y, z_lo), goods: 16 (over x, z_hi, core).
Axes of the slice: x: 4, y: 4, z: 16 (z_hi: 2, z_lo: 8; z = z_hi * 8 + z_lo), core: 2. Of those that a mesh axis runs over, the one named last changes fastest.
Arguments:
- buyer_hidden: bfloat16 [40960, 1024], P('buyers', 'goods'), may hold values from -6 to 6
- goods_hidden: bfloat16 [32768, 1024], P('goods', 'buyers'), may hold values from -6 to 6
- buyer_proj: bfloat16 [1024, 128], replicated, may hold values from -0.1875 to 0.1875
- goods_proj: bfloat16 [1024, 128], replicated, may hold values from -0.1875 to 0.1875
- endowment: float32 [40960], P('buyers'), may hold values from 0.5 to 4
Outputs:
- prices: float32 [32768], P('goods')
- utility: float32 [40960], P('buyers')
All inputs are finite; a program needn't handle non-finite values.
Results may differ from a plain program's by a relative error of at most 0.0003.
The roundings to bfloat16 on the way count: a program that leaves them out, or rounds other values in their place, can miss the bound.
Values may be sent and summed in bfloat16 or wider, within the bound.
No kernel may reach another device: no remote copies, remote signals or barrier semaphores. Data moves between devices by JAX's collectives and lax.ppermute only.
A program may use at most 64 MiB of HBM per device.

v0:
```python
import jax
import jax.numpy as jnp
from jax import lax
from jax.sharding import PartitionSpec as P

E = 128
ITERS = 3


def per_device(buyer_hidden, goods_hidden, buyer_proj, goods_proj, endowment):
    proj_rows = buyer_proj
    buyer_sum = jnp.dot(
        lax.all_gather(buyer_hidden, "goods", axis=1, tiled=True),
        proj_rows,
        preferred_element_type=jnp.float32,
    )
    proj_rows = goods_proj
    goods_sum = jnp.dot(
        lax.all_gather(goods_hidden, "buyers", axis=1, tiled=True),
        proj_rows,
        preferred_element_type=jnp.float32,
    )
    buyer_emb = buyer_sum.astype(jnp.bfloat16)
    goods_emb = goods_sum.astype(jnp.bfloat16)
    scores = lax.dot_general(
        buyer_emb, goods_emb, (((1,), (1,)), ((), ())), preferred_element_type=jnp.float32
    )
    values = jax.nn.softplus(scores * E ** (-0.5)).astype(jnp.bfloat16)
    spread = lax.psum(jnp.sum(values, axis=1, dtype=jnp.float32), "goods")
    bid_block = (endowment / spread)[:, None] * values
    prices = spread
    utility = spread
    for repeat in range(ITERS):
        prices = lax.psum(jnp.sum(bid_block, 0), "buyers")
        shares = bid_block / prices[None, :]
        utility = lax.psum(jnp.sum(values * shares, 1), "goods")
        if repeat + 1 < ITERS:
            bid_block = (endowment / utility)[:, None] * values * shares
    return (prices, utility)


def solution(mesh):
    placed = (P("buyers", "goods"), P("goods", "buyers"), P(), P(), P("buyers"))
    return jax.shard_map(
        per_device, mesh=mesh, in_specs=placed, out_specs=(P("goods"), P("buyers")), check_vma=False
    )
```

profile of v0, /device:TPU:1, one launch (start us, length us, event | category | flops | bytes accessed | tf_op | source)
XLA Modules:
  0.0 1007.6 jit_solution(11603073471808425015)
XLA Ops:
  7.2 0.0 copy-start
  7.2 0.0 all-gather.5.cloned.1.call-start
  7.2 0.7 all-gather.5.cloned.1.call-update
  7.9 0.0 all-gather.3.cloned.1.call-start
  8.0 0.7 all-gather.3.cloned.1.call-update
  8.7 223.9 %all-gather.5.cloned.1.call-done = bf16[2048,1024]{0,1:T(8,128)(2,1)} async-done(((bf16[2048,32]{0,1:T(8,128)(2,1)}), bf16[2048,1024]{0,1:T(8,128)(2,1)}) %all-gather.5.cloned.1.call-update) | async-done | bytes 4194320 | tf_op jit(solution)/shard_map/all_gather | solution.py:19
  232.5 3.5 convolution_convert_fusion
  236.1 0.0 copy-start.1
  236.1 117.2 %all-gather.3.cloned.1.call-done = bf16[1280,1024]{0,1:T(8,128)(2,1)} async-done(((bf16[1280,64]{0,1:T(8,128)(2,1)}), bf16[1280,1024]{0,1:T(8,128)(2,1)}) %all-gather.3.cloned.1.call-update) | async-done | bytes 2621456 | tf_op jit(solution)/shard_map/all_gather | solution.py:13
  353.3 0.0 copy-done
  353.3 11.8 %convert_reduce_fusion = (f32[1280]{0:T(1024)S(1)}, bf16[1280,2048]{1,0:T(8,128)(2,1)}) fusion(bf16[2048,128]{1,0:T(8,128)(2,1)S(1)} %convolution_convert_fusion, bf16[1280,1024]{0,1:T(8,128)(2,1)} %all-gather.3.cloned.1.call-done, bf16[1024,128]{1,0:T(8,128)(2,1)S(1)} %copy-done), kind=kOutput, calls=%fused_computation.7 | convolution fusion | flops 1033009920 | bytes 8655872 | tf_op jit(solution)/shard_map/dot_general | solution.py:25
  365.2 62.1 %psum.49 = f32[1280]{0:T(1024)S(1)} all-reduce(f32[1280]{0:T(1024)S(1)} %get-tuple-element.2), channel_id=1, replica_groups=mesh['buyers'=32,'goods'=16] {'goods'}, use_global_device_ids=true, to_apply=%region_1.2 | all-reduce | flops 1280 | bytes 10240 | tf_op jit(solution)/shard_map/psum | solution.py:29
  427.3 0.0 copy-done.1
  427.3 3.6 fusion.1
  430.9 101.5 %psum.50 = f32[2048]{0:T(1024)S(1)} all-reduce(f32[2048]{0:T(1024)S(1)} %fusion.1), channel_id=1, replica_groups=mesh['buyers'=32,'goods'=16] {'buyers'}, use_global_device_ids=true, to_apply=%region_3.4 | all-reduce | flops 2048 | bytes 16384 | tf_op jit(solution)/shard_map/psum | solution.py:34
  532.3 4.4 fusion.2
  536.7 84.0 %psum.51 = f32[1280]{0:T(1024)S(1)} all-reduce(f32[1280]{0:T(1024)S(1)} %fusion.2), channel_id=1, replica_groups=mesh['buyers'=32,'goods'=16] {'goods'}, use_global_device_ids=true, to_apply=%region_5.6 | all-reduce | flops 1280 | bytes 10240 | tf_op jit(solution)/shard_map/psum | solution.py:36
  620.7 4.7 fusion.9
  625.5 101.0 %psum.52 = f32[2048]{0:T(1024)S(1)} all-reduce(f32[2048]{0:T(1024)S(1)} %fusion.9), channel_id=1, replica_groups=mesh['buyers'=32,'goods'=16] {'buyers'}, use_global_device_ids=true, to_apply=%region_7.8 | all-reduce | flops 2048 | bytes 16384 | tf_op jit(solution)/shard_map/psum | solution.py:34
  726.5 4.9 fusion.4
  731.4 76.3 %psum.53 = f32[1280]{0:T(1024)S(1)} all-reduce(f32[1280]{0:T(1024)S(1)} %fusion.4), channel_id=1, replica_groups=mesh['buyers'=32,'goods'=16] {'goods'}, use_global_device_ids=true, to_apply=%region_9.10 | all-reduce | flops 1280 | bytes 10240 | tf_op jit(solution)/shard_map/psum | solution.py:36
  807.7 6.5 fusion.8
  814.2 102.8 %psum.54 = f32[2048]{0:T(1024)S(1)} all-reduce(f32[2048]{0:T(1024)S(1)} %fusion.8), channel_id=1, replica_groups=mesh['buyers'=32,'goods'=16] {'buyers'}, use_global_device_ids=true, to_apply=%region_11.12 | all-reduce | flops 2048 | bytes 16384 | tf_op jit(solution)/shard_map/psum | solution.py:34
  917.0 0.0 copy-start.2
  917.0 6.5 fusion.6
  923.5 77.4 %psum.55 = f32[1280]{0:T(1024)} all-reduce(f32[1280]{0:T(1024)S(1)} %fusion.6), channel_id=1, replica_groups=mesh['buyers'=32,'goods'=16] {'goods'}, use_global_device_ids=true, to_apply=%region_13.14 | all-reduce | flops 1280 | bytes 10240 | tf_op jit(solution)/shard_map/psum | solution.py:36
  1000.8 0.0 copy-done.2
  (3 shorter events, 0.0 us)
Async XLA Ops:
  7.2 346.2 %copy-start = (bf16[1024,128]{1,0:T(8,128)(2,1)S(1)}, bf16[1024,128]{1,0:T(8,128)(2,1)}, u32[]{:S(2)}) copy-start(bf16[1024,128]{1,0:T(8,128)(2,1)} %param.7) | copy-start | bytes 786436
  7.2 225.4 %all-gather.5.cloned.1.call-start = ((), (), s32[]{:S(2)}) async-start(), calls=%async_computation.1 | async-start | bytes 4325376 | tf_op jit(solution)/shard_map/all_gather | solution.py:19
  7.9 345.4 %all-gather.3.cloned.1.call-start = ((), (), s32[]{:S(2)}) async-start(), calls=%async_computation | async-start | bytes 2785280 | tf_op jit(solution)/shard_map/all_gather | solution.py:13
  236.1 191.2 %copy-start.1 = (f32[1280]{0:T(1024)S(1)}, f32[1280]{0:T(1024)}, u32[]{:S(2)}) copy-start(f32[1280]{0:T(1024)} %param.9) | copy-start | bytes 15364
  917.0 83.8 %copy-start.2 = (f32[2048]{0:T(1024)}, f32[2048]{0:T(1024)S(1)}, u32[]{:S(2)}) copy-start(f32[2048]{0:T(1024)S(1)} %psum.54) | copy-start | bytes 24580
Sparse Core Ops, SparseCore 0:
  10.1 222.4 all-gather.4
  235.8 117.4 all-gather.2
where the time goes:
time: 1010 us
  blocking collectives  605 us (60%)
  waiting for transfers between devices  343 us (34%)
  other arithmetic  30.6 us (3%)
  matrix products  15.3 us (2%)
  between operations  14.2 us (1%)
    psum x3, blocking collectives, per_device(): prices = lax.psum(jnp.sum(bid_block, 0), 'buyers')  305 us
    psum x3, blocking collectives, per_device(): utility = lax.psum(jnp.sum(values * shares, 1), 'goods')  238 us
    all_gather x1, waiting for transfers between devices, per_device(): lax.all_gather(goods_hidden, 'buyers', axis=1, tiled=True)  224 us
    all_gather x1, waiting for transfers between devices, per_device(): lax.all_gather(buyer_hidden, 'goods', axis=1, tiled=True)  117 us
    psum x1, blocking collectives, per_device(): spread = lax.psum(jnp.sum(values, axis=1, dtype=jnp.float32), 'goods')  62.1 us
  transfers between devices with their start and end apart: 2, of which 2 were waited for; matrix products, arithmetic and copies ran while one was open for 0% of the time, Pallas kernels for 0%

commit v1 on v0

--- a/solution.py
+++ b/solution.py
@@ -7,12 +7,15 @@
 ITERS = 3
 
 
+def all_by_exchange(x, axis, dim):
+    sent = jnp.stack([x] * lax.axis_size(axis))
+    return jnp.concatenate(lax.all_to_all(sent, axis, 0, 0), axis=dim)
+
+
 def per_device(buyer_hidden, goods_hidden, buyer_proj, goods_proj, endowment):
     proj_rows = buyer_proj
     buyer_sum = jnp.dot(
-        lax.all_gather(buyer_hidden, "goods", axis=1, tiled=True),
-        proj_rows,
-        preferred_element_type=jnp.float32,
+        all_by_exchange(buyer_hidden, "goods", 1), proj_rows, preferred_element_type=jnp.float32
     )
     proj_rows = goods_proj
     goods_sum = jnp.dot(

time: 1010 us -> 966 us (0.956)
  waiting for transfers between devices: 343 us -> 266 us
  starting transfers between devices: 0.08 us -> 19.1 us
  blocking collectives: 605 us -> 617 us
    all_gather x1 -> x0, waiting for transfers between devices: 117 us -> none  [per_device(): lax.all_gather(buyer_hidden, 'goods', axis=1, tiled=True)]
    all_gather x1, waiting for transfers between devices: 224 us -> 266 us  [per_device(): lax.all_gather(goods_hidden, 'buyers', axis=1, tiled=True)]
    all_to_all x0 -> x1, starting transfers between devices: none -> 19.1 us  [all_by_exchange(): return jnp.concatenate(lax.all_to_all(sent, axis, 0, 0), axis=dim)]
    psum x1, blocking collectives: 62.1 us -> 76.7 us  [per_device(): spread = lax.psum(jnp.sum(values, axis=1, dtype=jnp.float32), 'goods')]
  transfers between devices with their start and end apart: 2 -> 2, of which waited for: 2 -> 1; matrix products, arithmetic and copies ran while one was open for 0% -> 0% of each run, Pallas kernels for 0% -> 0%
where the time goes in v1:
time: 966 us
  blocking collectives  617 us (64%)
  waiting for transfers between devices  266 us (28%)
  other arithmetic  30.5 us (3%)
  starting transfers between devices  19.1 us (2%)
  matrix products  15.9 us (2%)
  between operations  14.2 us (1%)
    psum x3, blocking collectives, per_device(): prices = lax.psum(jnp.sum(bid_block, 0), 'buyers')  310 us
    all_gather x1, waiting for transfers between devices, per_device(): lax.all_gather(goods_hidden, 'buyers', axis=1, tiled=True)  266 us
    psum x3, blocking collectives, per_device(): utility = lax.psum(jnp.sum(values * shares, 1), 'goods')  230 us
    psum x1, blocking collectives, per_device(): spread = lax.psum(jnp.sum(values, axis=1, dtype=jnp.float32), 'goods')  76.7 us
  transfers between devices with their start and end apart: 2, of which 1 were waited for; matrix products, arithmetic and copies ran while one was open for 0% of the time, Pallas kernels for 0%

profile of v1, /device:TPU:1, one launch (start us, length us, event | category | flops | bytes accessed | tf_op | source)
XLA Modules:
  0.0 965.8 jit_solution(1151589199503480627)
XLA Ops:
  7.2 0.0 copy-start
  7.2 0.0 copy-start.3
  7.2 2.8 stack.2
  9.9 19.1 %all-to-all-start = ((bf16[16,1280,64]{1,2,0:T(8,128)(2,1)}), bf16[16,1280,64]{1,2,0:T(8,128)(2,1)S(1)}, u32[]{:S(2)}, u32[]{:S(2)}) async-start(bf16[16,1280,64]{1,2,0:T(8,128)(2,1)} %stack.2), calls=%async_computation | async-start | bytes 5242880 | tf_op jit(solution)/shard_map/all_to_all | solution.py:12
  29.0 0.0 all-gather.2.cloned.1.call-start
  29.0 0.7 all-gather.2.cloned.1.call-update
  29.7 265.8 %all-gather.2.cloned.1.call-done = bf16[2048,1024]{0,1:T(8,128)(2,1)} async-done(((bf16[2048,32]{0,1:T(8,128)(2,1)}), bf16[2048,1024]{0,1:T(8,128)(2,1)}) %all-gather.2.cloned.1.call-update) | async-done | bytes 4194320 | tf_op jit(solution)/shard_map/all_gather | solution.py:22
  295.5 0.0 copy-done.3
  295.5 4.3 convolution_convert_fusion
  299.8 0.0 all-to-all-done
  299.8 0.0 copy-done
  299.8 0.0 copy-start.1
  299.9 11.6 %convert_reduce_fusion = (f32[1280]{0:T(1024)S(1)}, bf16[1280,2048]{1,0:T(8,128)(2,1)}) fusion(bf16[2048,128]{1,0:T(8,128)(2,1)} %convolution_convert_fusion, bf16[1280,1024]{0,1:T(8,128)(2,1)S(1)} %bitcast.8, bf16[1024,128]{1,0:T(8,128)(2,1)S(1)} %copy-done), kind=kOutput, calls=%fused_computation.7 | convolution fusion | flops 1033009920 | bytes 8655872 | tf_op jit(solution)/shard_map/dot_general | solution.py:28
  311.4 76.7 %psum.49 = f32[1280]{0:T(1024)S(1)} all-reduce(f32[1280]{0:T(1024)S(1)} %get-tuple-element.2), channel_id=1, replica_groups=mesh['buyers'=32,'goods'=16] {'goods'}, use_global_device_ids=true, to_apply=%region_1.2 | all-reduce | flops 1280 | bytes 10240 | tf_op jit(solution)/shard_map/psum | solution.py:32
  388.1 0.0 copy-done.1
  388.2 3.6 fusion.1
  391.8 106.0 %psum.50 = f32[2048]{0:T(1024)S(1)} all-reduce(f32[2048]{0:T(1024)S(1)} %fusion.1), channel_id=1, replica_groups=mesh['buyers'=32,'goods'=16] {'buyers'}, use_global_device_ids=true, to_apply=%region_3.4 | all-reduce | flops 2048 | bytes 16384 | tf_op jit(solution)/shard_map/psum | solution.py:37
  497.7 4.4 fusion.2
  502.1 76.9 %psum.51 = f32[1280]{0:T(1024)S(1)} all-reduce(f32[1280]{0:T(1024)S(1)} %fusion.2), channel_id=1, replica_groups=mesh['buyers'=32,'goods'=16] {'goods'}, use_global_device_ids=true, to_apply=%region_5.6 | all-reduce | flops 1280 | bytes 10240 | tf_op jit(solution)/shard_map/psum | solution.py:39
  579.0 4.7 fusion.9
  583.7 101.0 %psum.52 = f32[2048]{0:T(1024)S(1)} all-reduce(f32[2048]{0:T(1024)S(1)} %fusion.9), channel_id=1, replica_groups=mesh['buyers'=32,'goods'=16] {'buyers'}, use_global_device_ids=true, to_apply=%region_7.8 | all-reduce | flops 2048 | bytes 16384 | tf_op jit(solution)/shard_map/psum | solution.py:37
  684.7 4.9 fusion.4
  689.6 76.3 %psum.53 = f32[1280]{0:T(1024)S(1)} all-reduce(f32[1280]{0:T(1024)S(1)} %fusion.4), channel_id=1, replica_groups=mesh['buyers'=32,'goods'=16] {'goods'}, use_global_device_ids=true, to_apply=%region_9.10 | all-reduce | flops 1280 | bytes 10240 | tf_op jit(solution)/shard_map/psum | solution.py:39
  765.9 6.5 fusion.8
  772.4 102.7 %psum.54 = f32[2048]{0:T(1024)S(1)} all-reduce(f32[2048]{0:T(1024)S(1)} %fusion.8), channel_id=1, replica_groups=mesh['buyers'=32,'goods'=16] {'buyers'}, use_global_device_ids=true, to_apply=%region_11.12 | all-reduce | flops 2048 | bytes 16384 | tf_op jit(solution)/shard_map/psum | solution.py:37
  875.2 0.0 copy-start.2
  875.2 6.5 fusion.6
  881.7 77.3 %psum.55 = f32[1280]{0:T(1024)} all-reduce(f32[1280]{0:T(1024)S(1)} %fusion.6), channel_id=1, replica_groups=mesh['buyers'=32,'goods'=16] {'goods'}, use_global_device_ids=true, to_apply=%region_13.14 | all-reduce | flops 1280 | bytes 10240 | tf_op jit(solution)/shard_map/psum | solution.py:39
  959.0 0.0 copy-done.2
  (3 shorter events, 0.0 us)
Async XLA Ops:
  7.2 292.7 %copy-start = (bf16[1024,128]{1,0:T(8,128)(2,1)S(1)}, bf16[1024,128]{1,0:T(8,128)(2,1)}, u32[]{:S(2)}) copy-start(bf16[1024,128]{1,0:T(8,128)(2,1)} %param.7) | copy-start | bytes 786436
  7.2 288.3 %copy-start.3 = (bf16[1024,128]{1,0:T(8,128)(2,1)S(1)}, bf16[1024,128]{1,0:T(8,128)(2,1)}, u32[]{:S(2)}) copy-start(bf16[1024,128]{1,0:T(8,128)(2,1)} %param.8) | copy-start | bytes 786436
  9.9 289.9 %all-to-all-start = ((bf16[16,1280,64]{1,2,0:T(8,128)(2,1)}), bf16[16,1280,64]{1,2,0:T(8,128)(2,1)S(1)}, u32[]{:S(2)}, u32[]{:S(2)}) async-start(bf16[16,1280,64]{1,2,0:T(8,128)(2,1)} %stack.2), calls=%async_computation | async-start | bytes 5242880 | tf_op jit(solution)/shard_map/all_to_all | solution.py:12
  29.0 266.5 %all-gather.2.cloned.1.call-start = ((), (), s32[]{:S(2)}) async-start(), calls=%async_computation.1 | async-start | bytes 4325376 | tf_op jit(solution)/shard_map/all_gather | solution.py:22
  299.8 88.3 %copy-start.1 = (f32[1280]{0:T(1024)S(1)}, f32[1280]{0:T(1024)}, u32[]{:S(2)}) copy-start(f32[1280]{0:T(1024)} %param.9) | copy-start | bytes 15364
  875.2 83.8 %copy-start.2 = (f32[2048]{0:T(1024)}, f32[2048]{0:T(1024)S(1)}, u32[]{:S(2)}) copy-start(f32[2048]{0:T(1024)S(1)} %psum.54) | copy-start | bytes 24580
Sparse Core Ops, SparseCore 0:
  31.9 263.5 all-gather.1
